TPU v7x, 256 devices: a whole 4x4x8 slice. The times are simulated.
256 devices in a mesh: px: 32 (over z, x), py: 8 (over y, core).
Axes of the slice: x: 4, y: 4, z: 8, core: 2. Of those that a mesh axis runs over, the one named last changes fastest.
Arguments:
- field: float32 [512, 512, 1024], P('px', 'py'), may hold values from -120 to 120
- seeds_first: int32 [512, 128], replicated, may hold values from -64 to 63
- seeds_second: int32 [512, 128], replicated, may hold values from -64 to 63
Outputs:
- basis_first: float32 [512, 128], replicated
- basis_second: float32 [512, 128], replicated
- core_tensor: float32 [128, 128, 1024], P('px', 'py')
All inputs are finite; a program needn't handle non-finite values.
Results may differ from a plain program's by a relative error of at most 0.0003.
Values sent between devices are 32-bit elements; how exact they have to be, the bound alone decides.
No kernel may reach another device: no remote copies, remote signals or barrier semaphores. Data moves between devices by JAX's collectives and lax.ppermute only.
A program may use at most 128 MiB of HBM per device.

v0:
```python
import jax
import jax.numpy as jnp
from jax import lax
from jax.sharding import PartitionSpec as P

ITERS = 4


def orthonormal(matrix):
    inner = jnp.dot(matrix.T, matrix, precision=lax.Precision.HIGHEST)
    factor = jnp.linalg.cholesky(inner)
    return jax.scipy.linalg.solve_triangular(factor, matrix.T, lower=True).T


def leading_basis(partial_gram, seeds):
    basis = orthonormal(seeds.astype(jnp.float32))
    gram = lax.psum(partial_gram, ("px", "py"))
    for sweep in range(ITERS):
        basis = orthonormal(jnp.dot(gram, basis, precision=lax.Precision.HIGHEST))
    return basis


def local(field, seeds_first, seeds_second):
    fibers = lax.all_to_all(field, "px", split_axis=1, concat_axis=0, tiled=True)
    whole_first = fibers.shape[0]
    flattened = fibers.reshape(whole_first, -1)
    partial_first = jnp.dot(flattened, flattened.T, precision=lax.Precision.HIGHEST)
    basis_first = leading_basis(partial_first, seeds_first)
    rank_size = basis_first.shape[1]
    reduced = jnp.dot(basis_first.T, flattened, precision=lax.Precision.HIGHEST)
    reduced = reduced.reshape(rank_size, fibers.shape[1], fibers.shape[2])
    slab_fibers = lax.all_to_all(
        lax.all_to_all(reduced, "px", split_axis=0, concat_axis=1, tiled=True),
        "py",
        split_axis=2,
        concat_axis=1,
        tiled=True,
    )
    whole_second = slab_fibers.shape[1]
    turned = jnp.transpose(slab_fibers, (1, 0, 2)).reshape(whole_second, -1)
    partial_second = jnp.dot(turned, turned.T, precision=lax.Precision.HIGHEST)
    basis_second = leading_basis(partial_second, seeds_second)
    core_tensor = jnp.einsum(
        "jb,ajp->abp", basis_second, slab_fibers, precision=lax.Precision.HIGHEST
    )
    core_tensor = lax.all_to_all(core_tensor, "py", split_axis=1, concat_axis=2, tiled=True)
    return (basis_first, basis_second, core_tensor)


def solution(mesh):
    placed = (P("px", "py", None), P(), P())
    return jax.shard_map(
        local,
        mesh=mesh,
        in_specs=placed,
        out_specs=(P(), P(), P("px", "py", None)),
        check_vma=False,
    )
```

profile of v0, /device:TPU:1, one launch (start us, length us, event | category | flops | bytes accessed | tf_op | source)
XLA Modules:
  0.0 948.8 jit_solution(8441352326940024443)
XLA Ops:
  7.2 6.6 copy.84
  13.8 12.1 %all-to-all-start = ((f32[16,64,1024]{2,0,1:T(8,128)}), f32[16,64,1024]{2,0,1:T(8,128)}, u32[]{:S(2)}, u32[]{:S(2)}) async-start(f32[16,64,1024]{2,0,1:T(8,128)} %copy.84), calls=%async_computation | async-start | bytes 8388608 | tf_op jit(solution)/shard_map/all_to_all | solution.py:24
  27.0 11.7 %cholesky.164 = f32[128,128]{1,0:T(8,128)S(1)} custom-call(f32[128,128]{1,0:T(8,128)S(1)} %fusion.58), custom_call_target="Cholesky" | custom-call | tf_op jit(solution)/shard_map/jit(cholesky)/cholesky | solution.py:11
  38.7 80.2 %all-to-all-done = f32[16,64,1024]{2,0,1:T(8,128)} async-done(((f32[16,64,1024]{2,0,1:T(8,128)}), f32[16,64,1024]{2,0,1:T(8,128)}, u32[]{:S(2)}, u32[]{:S(2)}) %all-to-all-start) | async-done | bytes 4194336 | tf_op jit(solution)/shard_map/all_to_all | solution.py:24
  118.9 5.5 copy.85
  128.4 8.4 fusion.67
  138.1 9.8 %custom-call.14 = f32[1,128,128]{1,2,0:T(8,128)S(1)} custom-call(f32[1,128,128]{2,1,0:T(8,128)S(1)} %fusion.29), custom_call_target="InvertDiagBlocksLowerTriangular" | custom-call | tf_op jit(solution)/shard_map/jit(_solve_triangular)/triangular_solve | solution.py:12
  148.3 5.5 copy.91
  153.9 237.6 %all-reduce.3.cloned.1.call-done = f32[512,512]{1,0:T(8,128)} async-done(((f32[512,512]{1,0:T(8,128)}), f32[512,512]{1,0:T(8,128)}) %all-reduce.3.cloned.1.call-update) | async-done | bytes 1048592 | tf_op jit(solution)/shard_map/psum | solution.py:17
  394.5 11.7 %cholesky.175 = f32[128,128]{1,0:T(8,128)S(1)} custom-call(f32[128,128]{1,0:T(8,128)S(1)} %fusion.56), custom_call_target="Cholesky" | custom-call | tf_op jit(solution)/shard_map/jit(cholesky)/cholesky | solution.py:11
  407.6 9.8 %custom-call.15 = f32[1,128,128]{1,2,0:T(8,128)S(1)} custom-call(f32[1,128,128]{2,1,0:T(8,128)S(1)} %fusion.30), custom_call_target="InvertDiagBlocksLowerTriangular" | custom-call | tf_op jit(solution)/shard_map/jit(_solve_triangular)/triangular_solve | solution.py:12
  420.8 11.9 %cholesky.186 = f32[128,128]{1,0:T(8,128)S(1)} custom-call(f32[128,128]{1,0:T(8,128)S(1)} %fusion.54), custom_call_target="Cholesky" | custom-call | tf_op jit(solution)/shard_map/jit(cholesky)/cholesky | solution.py:11
  434.0 9.8 %custom-call.16 = f32[1,128,128]{1,2,0:T(8,128)S(1)} custom-call(f32[1,128,128]{2,1,0:T(8,128)S(1)} %fusion.31), custom_call_target="InvertDiagBlocksLowerTriangular" | custom-call | tf_op jit(solution)/shard_map/jit(_solve_triangular)/triangular_solve | solution.py:12
  446.0 11.7 %cholesky.197 = f32[128,128]{1,0:T(8,128)S(1)} custom-call(f32[128,128]{1,0:T(8,128)S(1)} %fusion.52), custom_call_target="Cholesky" | custom-call | tf_op jit(solution)/shard_map/jit(cholesky)/cholesky | solution.py:11
  459.0 9.8 %custom-call.17 = f32[1,128,128]{1,2,0:T(8,128)S(1)} custom-call(f32[1,128,128]{2,1,0:T(8,128)S(1)} %fusion.32), custom_call_target="InvertDiagBlocksLowerTriangular" | custom-call | tf_op jit(solution)/shard_map/jit(_solve_triangular)/triangular_solve | solution.py:12
  471.3 11.7 %cholesky.208 = f32[128,128]{1,0:T(8,128)S(1)} custom-call(f32[128,128]{1,0:T(8,128)S(1)} %fusion.50), custom_call_target="Cholesky" | custom-call | tf_op jit(solution)/shard_map/jit(cholesky)/cholesky | solution.py:11
  484.4 9.8 %custom-call.18 = f32[1,128,128]{1,2,0:T(8,128)S(1)} custom-call(f32[1,128,128]{2,1,0:T(8,128)S(1)} %fusion.33), custom_call_target="InvertDiagBlocksLowerTriangular" | custom-call | tf_op jit(solution)/shard_map/jit(_solve_triangular)/triangular_solve | solution.py:12
  494.6 6.5 fusion.11
  502.1 35.5 %all_to_all.69 = f32[128,2,1024]{2,1,0:T(2,128)S(1)} all-to-all(f32[128,2,1024]{2,1,0:T(2,128)S(1)} %copy.92), channel_id=1, replica_groups=mesh['px'=32,'py'=8] {'px'}, dimensions={0} | all-to-all | bytes 2097152 | tf_op jit(solution)/shard_map/all_to_all | solution.py:33
  541.8 6.2 all-to-all-start.2
  548.8 11.7 %cholesky.219 = f32[128,128]{1,0:T(8,128)S(1)} custom-call(f32[128,128]{1,0:T(8,128)S(1)} %fusion.48), custom_call_target="Cholesky" | custom-call | tf_op jit(solution)/shard_map/jit(cholesky)/cholesky | solution.py:11
  573.5 9.8 %custom-call.19 = f32[1,128,128]{1,2,0:T(8,128)S(1)} custom-call(f32[1,128,128]{2,1,0:T(8,128)S(1)} %fusion.34), custom_call_target="InvertDiagBlocksLowerTriangular" | custom-call | tf_op jit(solution)/shard_map/jit(_solve_triangular)/triangular_solve | solution.py:12
  583.8 238.5 %all-reduce.5.cloned.1.call-done = f32[512,512]{1,0:T(8,128)} async-done(((f32[512,512]{1,0:T(8,128)}), f32[512,512]{1,0:T(8,128)}) %all-reduce.5.cloned.1.call-update) | async-done | bytes 1048592 | tf_op jit(solution)/shard_map/psum | solution.py:17
  825.2 11.7 %cholesky.230 = f32[128,128]{1,0:T(8,128)S(1)} custom-call(f32[128,128]{1,0:T(8,128)S(1)} %fusion.46), custom_call_target="Cholesky" | custom-call | tf_op jit(solution)/shard_map/jit(cholesky)/cholesky | solution.py:11
  838.3 10.2 %custom-call.20 = f32[1,128,128]{1,2,0:T(8,128)S(1)} custom-call(f32[1,128,128]{2,1,0:T(8,128)S(1)} %fusion.35), custom_call_target="InvertDiagBlocksLowerTriangular" | custom-call | tf_op jit(solution)/shard_map/jit(_solve_triangular)/triangular_solve | solution.py:12
  851.8 11.7 %cholesky.241 = f32[128,128]{1,0:T(8,128)S(1)} custom-call(f32[128,128]{1,0:T(8,128)S(1)} %fusion.44), custom_call_target="Cholesky" | custom-call | tf_op jit(solution)/shard_map/jit(cholesky)/cholesky | solution.py:11
  864.9 9.8 %custom-call.21 = f32[1,128,128]{1,2,0:T(8,128)S(1)} custom-call(f32[1,128,128]{2,1,0:T(8,128)S(1)} %fusion.36), custom_call_target="InvertDiagBlocksLowerTriangular" | custom-call | tf_op jit(solution)/shard_map/jit(_solve_triangular)/triangular_solve | solution.py:12
  876.8 11.9 %cholesky.252 = f32[128,128]{1,0:T(8,128)S(1)} custom-call(f32[128,128]{1,0:T(8,128)S(1)} %fusion.42), custom_call_target="Cholesky" | custom-call | tf_op jit(solution)/shard_map/jit(cholesky)/cholesky | solution.py:11
  890.0 9.8 %custom-call.22 = f32[1,128,128]{1,2,0:T(8,128)S(1)} custom-call(f32[1,128,128]{2,1,0:T(8,128)S(1)} %fusion.37), custom_call_target="InvertDiagBlocksLowerTriangular" | custom-call | tf_op jit(solution)/shard_map/jit(_solve_triangular)/triangular_solve | solution.py:12
  902.0 11.7 %cholesky.263 = f32[128,128]{1,0:T(8,128)S(1)} custom-call(f32[128,128]{1,0:T(8,128)S(1)} %fusion.40), custom_call_target="Cholesky" | custom-call | tf_op jit(solution)/shard_map/jit(cholesky)/cholesky | solution.py:11
  915.0 10.0 %custom-call.23 = f32[1,128,128]{1,2,0:T(8,128)S(1)} custom-call(f32[1,128,128]{2,1,0:T(8,128)S(1)} %fusion.38), custom_call_target="InvertDiagBlocksLowerTriangular" | custom-call | tf_op jit(solution)/shard_map/jit(_solve_triangular)/triangular_solve | solution.py:12
  928.1 6.4 all-to-all-start.3
  (112 shorter events, 68.7 us)
Async XLA Ops:
  13.8 12.5 %copy-start.3 = (s32[512,128]{1,0:T(8,128)S(1)}, s32[512,128]{1,0:T(8,128)}, u32[]{:S(2)}) copy-start(s32[512,128]{1,0:T(8,128)} %param.7) | copy-start | bytes 786436
  13.8 105.2 %all-to-all-start = ((f32[16,64,1024]{2,0,1:T(8,128)}), f32[16,64,1024]{2,0,1:T(8,128)}, u32[]{:S(2)}, u32[]{:S(2)}) async-start(f32[16,64,1024]{2,0,1:T(8,128)} %copy.84), calls=%async_computation | async-start | bytes 8388608 | tf_op jit(solution)/shard_map/all_to_all | solution.py:24
  25.9 365.6 %all-reduce.3.cloned.1.call-start = ((), (), s32[]{:S(2)}) async-start(), calls=%async_computation.4 | async-start | bytes 2097152 | tf_op jit(solution)/shard_map/psum | solution.py:17
  126.4 1.9 copy-start
  391.5 52.7 %copy-start.1 = (f32[512,512]{1,0:T(8,128)S(1)}, f32[512,512]{1,0:T(8,128)}, u32[]{:S(2)}) copy-start(f32[512,512]{1,0:T(8,128)} %all-reduce.3.cloned.1.call-done) | copy-start | bytes 3145732
  539.0 9.0 copy-start.4
  541.8 21.3 %all-to-all-start.2 = ((f32[8,1,32768]{2,1,0:T(1,128)}), f32[8,1,32768]{2,1,0:T(1,128)S(1)}, u32[]{:S(2)}, u32[]{:S(2)}) async-start(f32[8,1,32768]{2,1,0:T(1,128)} %reshape.25), calls=%async_computation.2 | async-start | bytes 2097152 | tf_op jit(solution)/shard_map/all_to_all | solution.py:32
  548.1 274.2 %all-reduce.5.cloned.1.call-start = ((), (), s32[]{:S(2)}) async-start(), calls=%async_computation.5 | async-start | bytes 2097152 | tf_op jit(solution)/shard_map/psum | solution.py:17
  569.3 14.1 %copy-start.5 = (s32[512,128]{1,0:T(8,128)S(1)}, s32[512,128]{1,0:T(8,128)}, u32[]{:S(2)}) copy-start(s32[512,128]{1,0:T(8,128)} %param.8) | copy-start | bytes 786436
  822.2 52.9 %copy-start.2 = (f32[512,512]{1,0:T(8,128)S(1)}, f32[512,512]{1,0:T(8,128)}, u32[]{:S(2)}) copy-start(f32[512,512]{1,0:T(8,128)} %all-reduce.5.cloned.1.call-done) | copy-start | bytes 3145732
  928.1 12.9 %all-to-all-start.3 = ((f32[4,128,128]{2,0,1:T(4,128)}), f32[4,128,128]{2,0,1:T(4,128)S(1)}, u32[]{:S(2)}, u32[]{:S(2)}) async-start(f32[4,128,128]{2,0,1:T(4,128)} %copy.103), calls=%async_computation.3 | async-start | bytes 524288 | tf_op jit(solution)/shard_map/all_to_all | solution.py:46
Sparse Core Ops, SparseCore 0:
  136.9 254.5 all-reduce.2
  572.3 249.8 all-reduce.4
where the time goes:
time: 952 us; the launch traced here: 949 us
  waiting for transfers between devices  564 us (59%)
  other arithmetic  233 us (24%)
  matrix products  43 us (5%)
  blocking collectives  35.5 us (4%)
  local copies, waits for them, and re-layouts  33.7 us (4%)
  starting transfers between devices  25.1 us (3%)
  between operations  14.9 us (2%)
    psum x2, waiting for transfers between devices, leading_basis(): gram = lax.psum(partial_gram, ('px', 'py'))  476 us
    another operation x30, other arithmetic, orthonormal(): factor = jnp.linalg.cholesky(inner)  124 us
    another operation x20, other arithmetic, orthonormal(): return jax.scipy.linalg.solve_triangular(factor, matrix.T, lower=True).T  105 us
    all_to_all x1, waiting for transfers between devices, local(): lax.all_to_all(field, 'px', split_axis=1, concat_axis=0, tiled=True)  80.2 us
    all_to_all x1, blocking collectives, local(): lax.all_to_all(reduced, 'px', split_axis=0, concat_axis=1, tiled=True)  35.5 us
  transfers between devices with their start and end apart: 5, of which 5 were waited for; matrix products, arithmetic and copies ran while one was open for 6% of the time, Pallas kernels for 0%

commit v1 on v0

--- a/solution.py
+++ b/solution.py
@@ -14,7 +14,7 @@
 
 def leading_basis(partial_gram, seeds):
     basis = orthonormal(seeds.astype(jnp.float32))
-    gram = lax.psum(partial_gram, ("px", "py"))
+    gram = lax.psum(lax.psum(partial_gram, "px"), "py")
     for sweep in range(ITERS):
         basis = orthonormal(jnp.dot(gram, basis, precision=lax.Precision.HIGHEST))
     return basis

time: 952 us -> 868 us (0.912)
  waiting for transfers between devices: 564 us -> 376 us
  blocking collectives: 35.5 us -> 163 us
  starting transfers between devices: 25.1 us -> 6.37 us
    all_to_all x0 -> x2, blocking collectives: none -> 129 us  [the longest x1 105 us: local(): lax.all_to_all(field, 'px', split_axis=1, concat_axis=0, tiled=True)]
    psum x2 -> x4, waiting for transfers between devices: 476 us -> 371 us  [leading_basis(): gram = lax.psum(lax.psum(partial_gram, 'px'), 'py')]
    all_to_all x2 -> x0, waiting for transfers between devices: 82.9 us -> none  [the longest x1 80.2 us: local(): lax.all_to_all(field, 'px', split_axis=1, concat_axis=0, tiled=True)]
    all_to_all x2 -> x0, starting transfers between devices: 18.4 us -> none  [the longest x1 12.1 us: local(): lax.all_to_all(field, 'px', split_axis=1, concat_axis=0, tiled=True)]
where the time goes in v1:
time: 868 us; the launch traced here: 864 us
  waiting for transfers between devices  376 us (43%)
  other arithmetic  233 us (27%)
  blocking collectives  163 us (19%)
  matrix products  43.1 us (5%)
  local copies, waits for them, and re-layouts  28.6 us (3%)
  between operations  14.8 us (2%)
    psum x4, waiting for transfers between devices, leading_basis(): gram = lax.psum(lax.psum(partial_gram, 'px'), 'py')  371 us
    another operation x30, other arithmetic, orthonormal(): factor = jnp.linalg.cholesky(inner)  125 us
    all_to_all x1, blocking collectives, local(): lax.all_to_all(field, 'px', split_axis=1, concat_axis=0, tiled=True)  105 us
    another operation x20, other arithmetic, orthonormal(): return jax.scipy.linalg.solve_triangular(factor, matrix.T, lower=True).T  105 us
    all_to_all x1, blocking collectives, local(): lax.all_to_all(reduced, 'px', split_axis=0, concat_axis=1, tiled=True)  33.9 us
    all_to_all x1, blocking collectives, local(): lax.all_to_all(lax.all_to_all(reduced, 'px', split_axis=0, concat_axis=1,...  24.1 us
  transfers between devices with their start and end apart: 5, of which 5 were waited for; matrix products, arithmetic and copies ran while one was open for 6% of the time, Pallas kernels for 0%

profile of v1, /device:TPU:1, one launch (start us, length us, event | category | flops | bytes accessed | tf_op | source)
XLA Modules:
  0.0 864.5 jit_solution(15549265519671015609)
XLA Ops:
  11.8 105.3 %all_to_all.69 = f32[16,64,1024]{2,0,1:T(8,128)S(1)} all-to-all(f32[16,64,1024]{2,0,1:T(8,128)S(1)} %copy.84), channel_id=1, replica_groups=mesh['px'=32,'py'=8] {'px'}, dimensions={1} | all-to-all | bytes 8388608 | tf_op jit(solution)/shard_map/all_to_all | solution.py:24
  124.4 8.4 fusion.67
  133.6 11.7 %cholesky.164 = f32[128,128]{1,0:T(8,128)S(1)} custom-call(f32[128,128]{1,0:T(8,128)S(1)} %fusion.58), custom_call_target="Cholesky" | custom-call | tf_op jit(solution)/shard_map/jit(cholesky)/cholesky | solution.py:11
  145.4 131.9 %all-reduce.5.cloned.1.call-done = f32[512,512]{1,0:T(8,128)} async-done(((f32[512,512]{1,0:T(8,128)}), f32[512,512]{1,0:T(8,128)}) %all-reduce.5.cloned.1.call-update) | async-done | bytes 1048592 | tf_op jit(solution)/shard_map/psum | solution.py:17
  278.6 9.8 %custom-call.14 = f32[1,128,128]{1,2,0:T(8,128)S(1)} custom-call(f32[1,128,128]{2,1,0:T(8,128)S(1)} %fusion.29), custom_call_target="InvertDiagBlocksLowerTriangular" | custom-call | tf_op jit(solution)/shard_map/jit(_solve_triangular)/triangular_solve | solution.py:12
  288.9 5.5 copy.91
  294.4 52.9 %all-reduce.7.cloned.1.call-done = f32[512,512]{1,0:T(8,128)} async-done(((f32[512,512]{1,0:T(8,128)}), f32[512,512]{1,0:T(8,128)}) %all-reduce.7.cloned.1.call-update) | async-done | bytes 1048592 | tf_op jit(solution)/shard_map/psum | solution.py:17
  350.3 11.7 %cholesky.175 = f32[128,128]{1,0:T(8,128)S(1)} custom-call(f32[128,128]{1,0:T(8,128)S(1)} %fusion.56), custom_call_target="Cholesky" | custom-call | tf_op jit(solution)/shard_map/jit(cholesky)/cholesky | solution.py:11
  363.3 9.8 %custom-call.15 = f32[1,128,128]{1,2,0:T(8,128)S(1)} custom-call(f32[1,128,128]{2,1,0:T(8,128)S(1)} %fusion.30), custom_call_target="InvertDiagBlocksLowerTriangular" | custom-call | tf_op jit(solution)/shard_map/jit(_solve_triangular)/triangular_solve | solution.py:12
  376.5 11.9 %cholesky.186 = f32[128,128]{1,0:T(8,128)S(1)} custom-call(f32[128,128]{1,0:T(8,128)S(1)} %fusion.54), custom_call_target="Cholesky" | custom-call | tf_op jit(solution)/shard_map/jit(cholesky)/cholesky | solution.py:11
  389.7 9.8 %custom-call.16 = f32[1,128,128]{1,2,0:T(8,128)S(1)} custom-call(f32[1,128,128]{2,1,0:T(8,128)S(1)} %fusion.31), custom_call_target="InvertDiagBlocksLowerTriangular" | custom-call | tf_op jit(solution)/shard_map/jit(_solve_triangular)/triangular_solve | solution.py:12
  401.7 11.7 %cholesky.197 = f32[128,128]{1,0:T(8,128)S(1)} custom-call(f32[128,128]{1,0:T(8,128)S(1)} %fusion.52), custom_call_target="Cholesky" | custom-call | tf_op jit(solution)/shard_map/jit(cholesky)/cholesky | solution.py:11
  414.7 9.8 %custom-call.17 = f32[1,128,128]{1,2,0:T(8,128)S(1)} custom-call(f32[1,128,128]{2,1,0:T(8,128)S(1)} %fusion.32), custom_call_target="InvertDiagBlocksLowerTriangular" | custom-call | tf_op jit(solution)/shard_map/jit(_solve_triangular)/triangular_solve | solution.py:12
  427.1 11.7 %cholesky.208 = f32[128,128]{1,0:T(8,128)S(1)} custom-call(f32[128,128]{1,0:T(8,128)S(1)} %fusion.50), custom_call_target="Cholesky" | custom-call | tf_op jit(solution)/shard_map/jit(cholesky)/cholesky | solution.py:11
  440.1 9.8 %custom-call.18 = f32[1,128,128]{1,2,0:T(8,128)S(1)} custom-call(f32[1,128,128]{2,1,0:T(8,128)S(1)} %fusion.33), custom_call_target="InvertDiagBlocksLowerTriangular" | custom-call | tf_op jit(solution)/shard_map/jit(_solve_triangular)/triangular_solve | solution.py:12
  450.4 6.5 fusion.11
  457.9 33.9 %all_to_all.70 = f32[128,2,1024]{2,1,0:T(2,128)S(1)} all-to-all(f32[128,2,1024]{2,1,0:T(2,128)S(1)} %copy.92), channel_id=1, replica_groups=mesh['px'=32,'py'=8] {'px'}, dimensions={0} | all-to-all | bytes 2097152 | tf_op jit(solution)/shard_map/all_to_all | solution.py:33
  495.1 24.1 %all_to_all.71 = f32[8,1,32768]{2,1,0:T(1,128)S(1)} all-to-all(f32[8,1,32768]{2,1,0:T(1,128)S(1)} %reshape.25), channel_id=1, replica_groups=mesh['px'=32,'py'=8] {'py'}, dimensions={0} | all-to-all | bytes 2097152 | tf_op jit(solution)/shard_map/all_to_all | solution.py:32
  528.9 11.7 %cholesky.219 = f32[128,128]{1,0:T(8,128)S(1)} custom-call(f32[128,128]{1,0:T(8,128)S(1)} %fusion.48), custom_call_target="Cholesky" | custom-call | tf_op jit(solution)/shard_map/jit(cholesky)/cholesky | solution.py:11
  540.7 128.0 %all-reduce.9.cloned.1.call-done = f32[512,512]{1,0:T(8,128)} async-done(((f32[512,512]{1,0:T(8,128)}), f32[512,512]{1,0:T(8,128)}) %all-reduce.9.cloned.1.call-update) | async-done | bytes 1048592 | tf_op jit(solution)/shard_map/psum | solution.py:17
  670.0 9.8 %custom-call.19 = f32[1,128,128]{1,2,0:T(8,128)S(1)} custom-call(f32[1,128,128]{2,1,0:T(8,128)S(1)} %fusion.34), custom_call_target="InvertDiagBlocksLowerTriangular" | custom-call | tf_op jit(solution)/shard_map/jit(_solve_triangular)/triangular_solve | solution.py:12
  680.2 58.3 %all-reduce.11.cloned.1.call-done = f32[512,512]{1,0:T(8,128)} async-done(((f32[512,512]{1,0:T(8,128)}), f32[512,512]{1,0:T(8,128)}) %all-reduce.11.cloned.1.call-update) | async-done | bytes 1048592 | tf_op jit(solution)/shard_map/psum | solution.py:17
  741.6 12.1 %cholesky.230 = f32[128,128]{1,0:T(8,128)S(1)} custom-call(f32[128,128]{1,0:T(8,128)S(1)} %fusion.46), custom_call_target="Cholesky" | custom-call | tf_op jit(solution)/shard_map/jit(cholesky)/cholesky | solution.py:11
  755.0 9.8 %custom-call.20 = f32[1,128,128]{1,2,0:T(8,128)S(1)} custom-call(f32[1,128,128]{2,1,0:T(8,128)S(1)} %fusion.35), custom_call_target="InvertDiagBlocksLowerTriangular" | custom-call | tf_op jit(solution)/shard_map/jit(_solve_triangular)/triangular_solve | solution.py:12
  768.2 11.7 %cholesky.241 = f32[128,128]{1,0:T(8,128)S(1)} custom-call(f32[128,128]{1,0:T(8,128)S(1)} %fusion.44), custom_call_target="Cholesky" | custom-call | tf_op jit(solution)/shard_map/jit(cholesky)/cholesky | solution.py:11
  781.2 9.8 %custom-call.21 = f32[1,128,128]{1,2,0:T(8,128)S(1)} custom-call(f32[1,128,128]{2,1,0:T(8,128)S(1)} %fusion.36), custom_call_target="InvertDiagBlocksLowerTriangular" | custom-call | tf_op jit(solution)/shard_map/jit(_solve_triangular)/triangular_solve | solution.py:12
  793.3 11.7 %cholesky.252 = f32[128,128]{1,0:T(8,128)S(1)} custom-call(f32[128,128]{1,0:T(8,128)S(1)} %fusion.42), custom_call_target="Cholesky" | custom-call | tf_op jit(solution)/shard_map/jit(cholesky)/cholesky | solution.py:11
  806.4 9.8 %custom-call.22 = f32[1,128,128]{1,2,0:T(8,128)S(1)} custom-call(f32[1,128,128]{2,1,0:T(8,128)S(1)} %fusion.37), custom_call_target="InvertDiagBlocksLowerTriangular" | custom-call | tf_op jit(solution)/shard_map/jit(_solve_triangular)/triangular_solve | solution.py:12
  818.3 11.9 %cholesky.263 = f32[128,128]{1,0:T(8,128)S(1)} custom-call(f32[128,128]{1,0:T(8,128)S(1)} %fusion.40), custom_call_target="Cholesky" | custom-call | tf_op jit(solution)/shard_map/jit(cholesky)/cholesky | solution.py:11
  831.6 9.8 %custom-call.23 = f32[1,128,128]{1,2,0:T(8,128)S(1)} custom-call(f32[1,128,128]{2,1,0:T(8,128)S(1)} %fusion.38), custom_call_target="InvertDiagBlocksLowerTriangular" | custom-call | tf_op jit(solution)/shard_map/jit(_solve_triangular)/triangular_solve | solution.py:12
  844.4 6.0 all-to-all-start.3
  852.1 4.9 all-to-all-done.3
  (114 shorter events, 68.2 us)
Async XLA Ops:
  7.2 270.1 %all-reduce.5.cloned.1.call-start = ((), (), s32[]{:S(2)}) async-start(), calls=%async_computation.4 | async-start | bytes 2097152 | tf_op jit(solution)/shard_map/psum | solution.py:17
  122.5 1.9 copy-start
  124.4 8.5 copy-start.3
  132.8 214.4 %all-reduce.7.cloned.1.call-start = ((), (), s32[]{:S(2)}) async-start(), calls=%async_computation.5 | async-start | bytes 2097152 | tf_op jit(solution)/shard_map/psum | solution.py:17
  277.3 391.4 %all-reduce.9.cloned.1.call-start = ((), (), s32[]{:S(2)}) async-start(), calls=%async_computation.6 | async-start | bytes 2097152 | tf_op jit(solution)/shard_map/psum | solution.py:17
  347.2 52.7 %copy-start.1 = (f32[512,512]{1,0:T(8,128)S(1)}, f32[512,512]{1,0:T(8,128)}, u32[]{:S(2)}) copy-start(f32[512,512]{1,0:T(8,128)} %all-reduce.7.cloned.1.call-done) | copy-start | bytes 3145732
  525.0 3.2 copy-start.4
  528.0 210.6 %all-reduce.11.cloned.1.call-start = ((), (), s32[]{:S(2)}) async-start(), calls=%async_computation.7 | async-start | bytes 2097152 | tf_op jit(solution)/shard_map/psum | solution.py:17
  738.5 52.9 %copy-start.2 = (f32[512,512]{1,0:T(8,128)S(1)}, f32[512,512]{1,0:T(8,128)}, u32[]{:S(2)}) copy-start(f32[512,512]{1,0:T(8,128)} %all-reduce.11.cloned.1.call-done) | copy-start | bytes 3145732
  844.4 12.5 %all-to-all-start.3 = ((f32[4,128,128]{2,0,1:T(4,128)}), f32[4,128,128]{2,0,1:T(4,128)S(1)}, u32[]{:S(2)}, u32[]{:S(2)}) async-start(f32[4,128,128]{2,0,1:T(4,128)} %copy.103), calls=%async_computation.3 | async-start | bytes 524288 | tf_op jit(solution)/shard_map/all_to_all | solution.py:46
Sparse Core Ops, SparseCore 0:
  133.0 144.2 all-reduce.4
  279.6 67.5 all-reduce.6
  528.1 140.5 all-reduce.8
  670.9 67.5 all-reduce.10
